TPU v7x, 128 devices: a whole 4x4x4 slice. The times are simulated.
128 devices in a mesh: vec: 8 (over y, z_lo), gz: 16 (over x, z_hi, core).
Axes of the slice: x: 4, y: 4, z: 4 (z_hi: 2, z_lo: 2; z = z_hi * 2 + z_lo), core: 2. Of those that a mesh axis runs over, the one named last changes fastest.
Arguments:
- vectors: bfloat16 [1024, 3, 2, 8192], P('vec', None, None, 'gz'), may hold values from -6 to 6
- links: float32 [3, 3, 3, 2, 8192], P(None, None, None, None, 'gz'), may hold values from -4 to 4
- dirs: int32 [6], replicated, may hold values from 0 to 5, each once
- moms: int32 [2, 3], replicated, may hold values from -2 to 2
Outputs:
- elementals: float32 [6, 2, 2, 1024, 1024], P(None, None, None, ('vec', 'gz'))
Inputs may be any that keep to these rules, and one draw needn't show every extreme that they name: `dirs`: each of the six directions appears exactly once.
All inputs are finite; a program needn't handle non-finite values.
Results may differ from a plain program's by a relative error of at most 0.0039.
Values may be sent and summed in bfloat16 or wider, within the bound.
A program may use at most 192 MiB of HBM per device.

v0:
```python
import math
import jax
import jax.numpy as jnp
from jax import lax
from jax.sharding import PartitionSpec as P

LX = 32
LY = 8


def colour_apply(link_real, link_imag, vec_real, vec_imag):
    out_real = jnp.float32(0.0)
    out_imag = jnp.float32(0.0)
    for column in range(3):
        left_real = link_real[None, :, column]
        left_imag = link_imag[None, :, column]
        right_real = vec_real[:, None, column].astype(jnp.float32)
        right_imag = vec_imag[:, None, column].astype(jnp.float32)
        out_real = out_real + left_real * right_real - left_imag * right_imag
        out_imag = out_imag + left_real * right_imag + left_imag * right_real
    return (out_real, out_imag)


def neighbour(field, stride, extent, position, forward):
    if forward:
        inside = jnp.roll(field, -stride, axis=-1)
        beside_all = jnp.roll(field, (extent - 1) * stride, axis=-1)
        return jnp.where(position == extent - 1, beside_all, inside)
    inside = jnp.roll(field, stride, axis=-1)
    beside_all = jnp.roll(field, -(extent - 1) * stride, axis=-1)
    return jnp.where(position == 0, beside_all, inside)


def on_device(vectors, links, dirs, moms):
    sites = vectors.shape[-1]
    plane = LY * LX
    depth = sites // plane
    shards = lax.axis_size("gz")
    flat = jnp.arange(sites, dtype=jnp.int32)
    x_index = flat % LX
    y_index = flat // LX % LY
    z_index = lax.axis_index("gz") * depth + flat // plane
    up = [(i, (i + 1) % shards) for i in range(shards)]
    down = [((i + 1) % shards, i) for i in range(shards)]
    gathered = lax.all_gather(vectors, "vec", axis=0, tiled=True)
    lower_links = lax.ppermute(links[2, :, :, :, sites - plane :], "gz", up)
    below = lax.ppermute(vectors[..., sites - plane :], "gz", up)
    above = lax.ppermute(vectors[..., :plane], "gz", down)
    momenta = moms.astype(jnp.float32)
    terms = []
    for direction in range(6):
        axis = direction % 3
        back = direction < 3
        step = -1 if back else 1
        link = links[axis]
        if axis == 0:
            moved = neighbour(vectors, 1, LX, x_index, not back)
            beside = neighbour(link, 1, LX, x_index, False) if back else link
        elif axis == 1:
            moved = neighbour(vectors, LX, LY, y_index, not back)
            beside = neighbour(link, LX, LY, y_index, False) if back else link
        elif back:
            moved = jnp.concatenate((below, vectors[..., : sites - plane]), axis=-1)
            beside = jnp.concatenate((lower_links, link[..., : sites - plane]), axis=-1)
        else:
            moved = jnp.concatenate((vectors[..., plane:], above), axis=-1)
            beside = link
        if back:
            link_real = jnp.swapaxes(beside[:, :, 0], 0, 1)
            link_imag = -jnp.swapaxes(beside[:, :, 1], 0, 1)
        else:
            link_real = beside[:, :, 0]
            link_imag = beside[:, :, 1]
        real, imag = colour_apply(link_real, link_imag, moved[:, :, 0], moved[:, :, 1])
        theta = (
            momenta[:, 0, None] * (x_index + (step if axis == 0 else 0)).astype(jnp.float32) / LX
            + momenta[:, 1, None] * (y_index + (step if axis == 1 else 0)).astype(jnp.float32) / LY
            + momenta[:, 2, None]
            * (z_index + (step if axis == 2 else 0)).astype(jnp.float32)
            / (depth * shards)
        ) * (2.0 * math.pi)
        cosine = jnp.cos(theta)[:, None, None]
        sine = jnp.sin(theta)[:, None, None]
        left_real = (cosine * real - sine * imag).astype(jnp.bfloat16)
        left_imag = (sine * real + cosine * imag).astype(jnp.bfloat16)
        left = jnp.stack(
            (jnp.stack((left_real, left_imag), axis=3), jnp.stack((-left_imag, left_real), axis=3)),
            axis=0,
        )
        product = jnp.einsum(
            "qpicrs,jcrs->pqij", left, gathered, preferred_element_type=jnp.float32
        )
        terms.append(lax.psum_scatter(product, "gz", scatter_dimension=2, tiled=True))
    stacked = jnp.stack(terms, axis=0)
    select = (dirs[:, None] == jnp.arange(6, dtype=jnp.int32)[None, :]).astype(jnp.float32)
    chosen = jnp.einsum("dk,kpqij->dpqij", select, stacked, precision=lax.Precision.HIGHEST)
    return chosen * (1.0 / math.sqrt(3.0 * sites * shards))


def solution(mesh):
    placed = (P("vec", None, None, "gz"), P(None, None, None, None, "gz"), P(), P())
    return jax.shard_map(
        on_device,
        mesh=mesh,
        in_specs=placed,
        out_specs=P(None, None, None, ("vec", "gz"), None),
        check_vma=False,
    )
```

profile of v0, /device:TPU:0, one launch (start us, length us, event | category | flops | bytes accessed | tf_op | source)
XLA Modules:
  0.0 600.4 jit_solution(9777820009141862032)
XLA Ops:
  6.5 2.1 copy.8
  8.7 2.0 fusion.148
  10.7 0.6 slice_bitcast_fusion.47
  11.3 4.1 collective-permute-start
  15.4 0.6 slice_bitcast_fusion.44
  16.0 0.7 slice.588
  16.7 0.6 slice.589
  17.3 0.7 slice.590
  18.5 1.0 fusion.129
  20.0 0.4 fusion.144
  20.4 0.4 fusion.147
  20.8 1.4 maximum_select_fusion
  22.4 0.6 multiply_subtract_fusion.5
  23.7 1.4 maximum_bitcast_fusion
  25.2 0.6 copy_bitcast_fusion.8
  25.9 0.7 fusion.149
  27.5 1.3 maximum_select_fusion.1
  28.8 1.0 slice_bitcast_fusion.5
  29.8 110.8 %all-gather.2.cloned.1.call-done = bf16[1024,3,2,512]{3,0,2,1:T(8,128)(2,1)} async-done(((bf16[128,3,2,512]{3,0,2,1:T(8,128)(2,1)}), bf16[1024,3,2,512]{3,0,2,1:T(8,128)(2,1)}) %all-gather.2.cloned.1.call-update) | async-done | bytes 6291472 | tf_op jit(solution)/shard_map/all_gather | solution.py:45
  140.6 8.1 %fusion.30 = f32[2,2,128,1024]{3,2,0,1:T(8,128)} fusion(bf16[1024,3,2,512]{3,0,2,1:T(8,128)(2,1)} %all-gather.2.cloned.1.call-done, bf16[1,2,128,3,2,512]{5,2,4,3,1,0:T(8,128)(2,1)} %get-tuple-element.83, bf16[1,2,128,3,2,512]{5,2,4,3,1,0:T(8,128)(2,1)S(1)} %get-tuple-element.82), kind=kOutput, calls=%fused_computation.30 | convolution fusion | flops 3222798336 | bytes 11534336 | tf_op jit(solution)/shard_map/qpicrs,jcrs->pqij/dot_general | solution.py:90
  149.0 0.4 copy-done.13
  149.4 0.6 slice.612
  150.0 0.6 copy.101
  150.7 0.7 sin.44
  151.6 0.6 multiply_subtract_fusion.4
  153.1 1.0 copy-done.5
  154.2 0.6 slice-done.1
  154.7 4.7 fusion.35
  159.6 0.6 copy-done.20
  160.2 0.8 fusion.103
  161.1 1.1 fusion.64
  162.4 0.6 multiply_subtract_fusion.3
  163.9 0.8 slice-done.2
  164.7 1.0 slice-done.3
  165.6 4.8 fusion.40
  171.4 0.6 multiply_subtract_fusion.2
  172.9 0.8 slice-done.4
  173.6 0.9 slice-done.5
  174.5 4.8 fusion.45
  179.4 0.7 copy-done.14
  180.5 0.6 multiply_subtract_fusion.1
  181.9 0.8 slice-done.6
  182.7 1.2 slice-done.7
  183.9 4.8 fusion.50
  188.7 4.4 collective-permute-start.2
  193.3 6.1 %collective-permute-done.2 = bf16[128,3,2,256]{3,0,2,1:T(8,128)(2,1)S(1)} collective-permute-done((bf16[128,3,2,256]{3,0,2,1:T(8,128)(2,1)S(1)}, bf16[128,3,2,256]{3,0,2,1:T(8,128)(2,1)S(1)}, u32[]{:S(2)}, u32[]{:S(2)}) %collective-permute-start.2) | collective-permute-done | bytes 393248 | tf_op jit(solution)/shard_map/ppermute | solution.py:48
  199.7 0.6 multiply_subtract_fusion
  201.1 0.8 slice-done.8
  201.9 0.9 slice-done.9
  202.8 4.7 fusion.55
  207.6 13.6 %reduce-scatter.7.cloned.1.call-done = f32[2,2,8,1024]{3,2,0,1:T(8,128)} async-done(((f32[2,2,128,1024]{3,2,0,1:T(8,128)}), f32[2,2,8,1024]{3,2,0,1:T(8,128)}) %reduce-scatter.7.cloned.1.call-update) | async-done | bytes 131088 | tf_op jit(solution)/shard_map/reduce_scatter | solution.py:93
  221.2 0.9 bitcast_dynamic-update-slice_fusion.5
  222.1 73.0 %reduce-scatter.9.cloned.1.call-done = f32[2,2,8,1024]{3,2,0,1:T(8,128)} async-done(((f32[2,2,128,1024]{3,2,0,1:T(8,128)}), f32[2,2,8,1024]{3,2,0,1:T(8,128)}) %reduce-scatter.9.cloned.1.call-update) | async-done | bytes 131088 | tf_op jit(solution)/shard_map/reduce_scatter | solution.py:93
  295.1 0.9 bitcast_dynamic-update-slice_fusion.4
  296.0 72.8 %reduce-scatter.11.cloned.1.call-done = f32[2,2,8,1024]{3,2,0,1:T(8,128)} async-done(((f32[2,2,128,1024]{3,2,0,1:T(8,128)}), f32[2,2,8,1024]{3,2,0,1:T(8,128)}) %reduce-scatter.11.cloned.1.call-update) | async-done | bytes 131088 | tf_op jit(solution)/shard_map/reduce_scatter | solution.py:93
  368.9 0.9 bitcast_dynamic-update-slice_fusion.3
  369.8 72.8 %reduce-scatter.13.cloned.1.call-done = f32[2,2,8,1024]{3,2,0,1:T(8,128)} async-done(((f32[2,2,128,1024]{3,2,0,1:T(8,128)}), f32[2,2,8,1024]{3,2,0,1:T(8,128)}) %reduce-scatter.13.cloned.1.call-update) | async-done | bytes 131088 | tf_op jit(solution)/shard_map/reduce_scatter | solution.py:93
  442.6 0.9 bitcast_dynamic-update-slice_fusion.2
  443.5 72.8 %reduce-scatter.15.cloned.1.call-done = f32[2,2,8,1024]{3,2,0,1:T(8,128)} async-done(((f32[2,2,128,1024]{3,2,0,1:T(8,128)}), f32[2,2,8,1024]{3,2,0,1:T(8,128)}) %reduce-scatter.15.cloned.1.call-update) | async-done | bytes 131088 | tf_op jit(solution)/shard_map/reduce_scatter | solution.py:93
  516.4 0.9 bitcast_dynamic-update-slice_fusion.1
  517.3 73.0 %reduce-scatter.17.cloned.1.call-done = f32[2,2,8,1024]{3,2,0,1:T(8,128)} async-done(((f32[2,2,128,1024]{3,2,0,1:T(8,128)}), f32[2,2,8,1024]{3,2,0,1:T(8,128)}) %reduce-scatter.17.cloned.1.call-update) | async-done | bytes 131088 | tf_op jit(solution)/shard_map/reduce_scatter | solution.py:93
  590.2 0.9 bitcast_dynamic-update-slice_fusion
  591.2 1.0 convolution_multiply_fusion
  592.2 1.3 copy.28
  (188 shorter events, 9.8 us)
Async XLA Ops:
  6.5 134.0 %all-gather.2.cloned.1.call-start = ((), (), s32[]{:S(2)}) async-start(), calls=%async_computation.6 | async-start | bytes 7077888 | tf_op jit(solution)/shard_map/all_gather | solution.py:45
  8.6 2.1 copy-start.10
  8.6 9.6 %copy-start.29 = (s32[2,3]{1,0:T(2,128)S(1)}, s32[2,3]{1,0:T(2,128)}, u32[]{:S(2)}) copy-start(s32[2,3]{1,0:T(2,128)} %param.7) | copy-start | bytes 76
  8.6 11.1 %copy-start = (bf16[128,3,2,512]{3,0,2,1:T(8,128)(2,1)S(1)}, bf16[128,3,2,512]{3,0,2,1:T(8,128)(2,1)}, u32[]{:S(2)}) copy-start(bf16[128,3,2,512]{3,0,2,1:T(8,128)(2,1)} %copy.8) | copy-start | bytes 2359300
  8.7 212.5 %reduce-scatter.7.cloned.1.call-start = ((), (), s32[]{:S(2)}) async-start(), calls=%async_computation.7 | async-start | bytes 2228224 | tf_op jit(solution)/shard_map/reduce_scatter | solution.py:93
  10.7 150.4 %collective-permute-start.1 = (bf16[128,3,2,256]{3,0,2,1:T(8,128)(2,1)S(1)}, bf16[128,3,2,256]{3,0,2,1:T(8,128)(2,1)}, u32[]{:S(2)}, u32[]{:S(2)}) collective-permute-start(bf16[128,3,2,256]{3,0,2,1:T(8,128)(2,1)S(1)} %get-tuple-element.76), channel_id=1, source_target_pairs={{0,1},{1,2},{2,3},{3,4},{4,5},{5,6},{6,7},{7,8},{8,9},{9,10},{10,1... | collective-permute-start | bytes 1179656 | tf_op jit(solution)/shard_map/ppermute | solution.py:47
  11.3 148.2 %collective-permute-start = (f32[3,3,2,256]{3,2,1,0:T(2,128)}, f32[3,3,2,256]{3,2,1,0:T(2,128)}, u32[]{:S(2)}, u32[]{:S(2)}) collective-permute-start(f32[3,3,2,256]{3,2,1,0:T(2,128)} %slice_bitcast_fusion.47), channel_id=1, source_target_pairs={{0,1},{1,2},{2,3},{3,4},{4,5},{5,6},{6,7},{7,8},{8,9},{9,10},{10,1... | collective-permute-start | bytes 55304 | tf_op jit(solution)/shard_map/ppermute | solution.py:46
  16.0 4.4 copy-start.4
  16.0 4.4 copy-start.6
  23.6 1.4 copy-start.7
  23.6 1.4 copy-start.11
  23.6 1.4 copy-start.19
  23.6 1.4 copy-start.23
  23.7 2.2 copy-start.8
  148.7 0.7 copy-start.13
  148.7 0.8 copy-start.9
  148.7 1.4 copy-start.18
  148.7 2.0 copy-start.28
  148.7 2.7 copy-start.27
  148.7 2.7 copy-start.12
  148.7 2.7 copy-start.3
  148.7 2.8 copy-start.2
  148.7 146.4 %reduce-scatter.9.cloned.1.call-start = ((), (), s32[]{:S(2)}) async-start(), calls=%async_computation.8 | async-start | bytes 2228224 | tf_op jit(solution)/shard_map/reduce_scatter | solution.py:93
  151.6 0.7 copy-start.21
  151.6 2.6 slice-start
  152.6 2.2 slice-start.1
  152.9 1.2 copy-start.5
  159.5 0.7 copy-start.20
  159.5 1.6 copy-start.1
  159.5 209.4 %reduce-scatter.11.cloned.1.call-start = ((), (), s32[]{:S(2)}) async-start(), calls=%async_computation.9 | async-start | bytes 2228224 | tf_op jit(solution)/shard_map/reduce_scatter | solution.py:93
  162.4 0.7 copy-start.22
  162.4 2.3 slice-start.2
  163.3 2.3 slice-start.3
  170.4 0.7 copy-start.26
  170.5 272.1 %reduce-scatter.13.cloned.1.call-start = ((), (), s32[]{:S(2)}) async-start(), calls=%async_computation.10 | async-start | bytes 2228224 | tf_op jit(solution)/shard_map/reduce_scatter | solution.py:93
  171.4 2.2 slice-start.4
  172.3 2.2 slice-start.5
  179.3 0.7 copy-start.14
  179.3 0.8 copy-start.17
  179.3 0.9 copy-start.25
  179.3 337.0 %reduce-scatter.15.cloned.1.call-start = ((), (), s32[]{:S(2)}) async-start(), calls=%async_computation.11 | async-start | bytes 2228224 | tf_op jit(solution)/shard_map/reduce_scatter | solution.py:93
  180.5 2.2 slice-start.6
  181.4 2.5 slice-start.7
  188.6 4.4 copy-start.16
  188.6 4.5 copy-start.15
  188.6 4.6 copy-start.24
  188.7 401.6 %reduce-scatter.17.cloned.1.call-start = ((), (), s32[]{:S(2)}) async-start(), calls=%async_computation.12 | async-start | bytes 2228224 | tf_op jit(solution)/shard_map/reduce_scatter | solution.py:93
  188.7 10.7 %collective-permute-start.2 = (bf16[128,3,2,256]{3,0,2,1:T(8,128)(2,1)S(1)}, bf16[128,3,2,256]{3,0,2,1:T(8,128)(2,1)S(1)}, u32[]{:S(2)}, u32[]{:S(2)}) collective-permute-start(bf16[128,3,2,256]{3,0,2,1:T(8,128)(2,1)S(1)} %copy-done.1), channel_id=1, source_target_pairs={{1,0},{2,1},{3,2},{4,3},{5,4},{6,5},{7,6},{8,7},{9,8},{10,9},{11,1... | collective-permute-start | bytes 1179656 | tf_op jit(solution)/shard_map/ppermute | solution.py:48
  199.7 2.2 slice-start.8
  200.6 2.2 slice-start.9
  207.5 383.6 %copy-start.30 = (s32[6]{0:T(128)S(1)}, s32[6]{0:T(128)}, u32[]{:S(2)}) copy-start(s32[6]{0:T(128)} %param.6) | copy-start | bytes 76
Sparse Core Ops, SparseCore 0:
  9.0 131.5 all-gather.1
  148.8 72.2 reduce-scatter.6
  225.1 69.9 reduce-scatter.8
  298.9 69.9 reduce-scatter.10
  372.7 69.9 reduce-scatter.12
  446.4 69.9 reduce-scatter.14
  520.3 69.8 reduce-scatter.16
where the time goes:
time: 601 us; the launch traced here: 600 us
  waiting for transfers between devices  495 us (82%)
  matrix products  32.9 us (5%)
  local copies, waits for them, and re-layouts  32.3 us (5%)
  other arithmetic  16.4 us (3%)
  between operations  14.6 us (2%)
  starting transfers between devices  9.11 us (2%)
    reduce_scatter x6, waiting for transfers between devices, on_device(): lax.psum_scatter(product, 'gz', scatter_dimension=2, tiled=True)  378 us
    all_gather x1, waiting for transfers between devices, on_device(): gathered = lax.all_gather(vectors, 'vec', axis=0, tiled=True)  111 us
    dot_general x6, matrix products, on_device(): jnp.einsum('qpicrs,jcrs->pqij', left, gathered, preferred_element_type=jn...  31.9 us
    unnamed x111, local copies, waits for them, and re-layouts  18.3 us
  transfers between devices with their start and end apart: 10, of which 8 were waited for; matrix products, arithmetic and copies ran while one was open for 11% of the time, Pallas kernels for 0%

commit v1 on v0

--- a/solution.py
+++ b/solution.py
@@ -42,7 +42,15 @@
     z_index = lax.axis_index("gz") * depth + flat // plane
     up = [(i, (i + 1) % shards) for i in range(shards)]
     down = [((i + 1) % shards, i) for i in range(shards)]
-    gathered = lax.all_gather(vectors, "vec", axis=0, tiled=True)
+    gathered = jnp.concatenate(
+        jax.lax.all_to_all(
+            jnp.stack([vectors for _ in range(jax.lax.axis_size("vec"))]),
+            split_axis=0,
+            concat_axis=0,
+            axis_name="vec",
+        ),
+        axis=0,
+    )
     lower_links = lax.ppermute(links[2, :, :, :, sites - plane :], "gz", up)
     below = lax.ppermute(vectors[..., sites - plane :], "gz", up)
     above = lax.ppermute(vectors[..., :plane], "gz", down)

time: 601 us -> 572 us (0.952)
  waiting for transfers between devices: 495 us -> 446 us
  starting transfers between devices: 9.11 us -> 19 us
  local copies, waits for them, and re-layouts: 32.3 us -> 41.8 us
    all_gather x1 -> x0, waiting for transfers between devices: 111 us -> none  [on_device(): gathered = lax.all_gather(vectors, 'vec', axis=0, tiled=True)]
    all_to_all x0 -> x1, waiting for transfers between devices: none -> 68.2 us  [on_device(): jax.lax.all_to_all(jnp.stack([vectors for _ in range(jax.lax.axis_size('v...]
    unnamed x111 -> x107, local copies, waits for them, and re-layouts: 18.3 us -> 21.5 us
  transfers between devices with their start and end apart: 10 -> 10, of which waited for: 8 -> 8; matrix products, arithmetic and copies ran while one was open for 11% -> 12% of each run, Pallas kernels for 0% -> 0%
where the time goes in v1:
time: 572 us; the launch traced here: 571 us
  waiting for transfers between devices  446 us (78%)
  local copies, waits for them, and re-layouts  41.8 us (7%)
  matrix products  29.7 us (5%)
  other arithmetic  19.4 us (3%)
  starting transfers between devices  19 us (3%)
  between operations  14.5 us (3%)
    reduce_scatter x6, waiting for transfers between devices, on_device(): lax.psum_scatter(product, 'gz', scatter_dimension=2, tiled=True)  373 us
    all_to_all x1, waiting for transfers between devices, on_device(): jax.lax.all_to_all(jnp.stack([vectors for _ in range(jax.lax.axis_size('v...  68.2 us
    dot_general x6, matrix products, on_device(): jnp.einsum('qpicrs,jcrs->pqij', left, gathered, preferred_element_type=jn...  28.6 us
    unnamed x107, local copies, waits for them, and re-layouts  21.5 us
  transfers between devices with their start and end apart: 10, of which 8 were waited for; matrix products, arithmetic and copies ran while one was open for 12% of the time, Pallas kernels for 0%

profile of v1, /device:TPU:0, one launch (start us, length us, event | category | flops | bytes accessed | tf_op | source)
XLA Modules:
  0.0 570.8 jit_solution(6875869718207664601)
XLA Ops:
  6.5 1.2 copy.29
  7.8 3.5 stack.151
  11.2 5.9 %all-to-all-start = ((bf16[8,128,3,2,512]{4,1,3,2,0:T(8,128)(2,1)}), bf16[8,128,3,2,512]{4,1,3,2,0:T(8,128)(2,1)}, u32[]{:S(2)}, u32[]{:S(2)}) async-start(bf16[8,128,3,2,512]{4,1,3,2,0:T(8,128)(2,1)} %stack.151), calls=%async_computation | async-start | bytes 12582912 | tf_op jit(solution)/shard_map/all_to_all | solution.py:46
  17.2 1.0 fusion.130
  18.2 0.6 slice_bitcast_fusion.47
  18.8 3.7 collective-permute-start
  22.8 0.6 slice_bitcast_fusion.44
  24.2 1.0 fusion.111
  26.0 1.4 maximum_select_fusion
  27.7 0.6 multiply_subtract_fusion.5
  28.9 1.8 maximum_bitcast_fusion
  30.9 0.6 copy_bitcast_fusion.8
  31.5 0.6 slice_bitcast_fusion.58
  32.1 0.6 copy_bitcast_fusion.4
  32.8 0.6 fusion.141
  33.4 0.8 fusion.123
  34.2 0.9 fusion.124
  35.1 1.3 fusion.125
  36.7 68.2 %all-to-all-done = bf16[8,128,3,2,512]{4,1,3,2,0:T(8,128)(2,1)} async-done(((bf16[8,128,3,2,512]{4,1,3,2,0:T(8,128)(2,1)}), bf16[8,128,3,2,512]{4,1,3,2,0:T(8,128)(2,1)}, u32[]{:S(2)}, u32[]{:S(2)}) %all-to-all-start) | async-done | bytes 6291488 | tf_op jit(solution)/shard_map/all_to_all | solution.py:46
  104.9 3.7 copy.34
  108.6 2.6 copy-done
  111.2 4.8 fusion.39
  116.8 0.6 slice.612
  117.4 0.7 sin.44
  118.1 0.6 copy.137
  118.7 2.6 maximum_select_fusion.1
  123.6 0.8 slice-done
  124.3 0.9 slice-done.1
  125.2 4.7 fusion.36
  130.0 0.6 copy-done.11
  130.7 0.8 fusion.85
  131.6 1.1 fusion.46
  132.9 0.6 multiply_subtract_fusion.3
  134.3 0.9 slice-done.2
  135.2 0.9 slice-done.3
  136.2 4.8 fusion.33
  144.2 0.8 slice-done.4
  145.0 0.9 slice-done.5
  145.8 4.7 fusion.30
  151.6 0.6 multiply_subtract_fusion.1
  153.0 0.9 slice-done.6
  153.9 1.0 slice-done.7
  154.9 4.8 fusion.27
  159.8 8.8 %collective-permute-start.2 = (bf16[128,3,2,256]{3,0,2,1:T(8,128)(2,1)S(1)}, bf16[128,3,2,256]{3,0,2,1:T(8,128)(2,1)S(1)}, u32[]{:S(2)}, u32[]{:S(2)}) collective-permute-start(bf16[128,3,2,256]{3,0,2,1:T(8,128)(2,1)S(1)} %copy-done.3), channel_id=1, source_target_pairs={{1,0},{2,1},{3,2},{4,3},{5,4},{6,5},{7,6},{8,7},{9,8},{10,9},{11,1... | collective-permute-start | bytes 1179656 | tf_op jit(solution)/shard_map/ppermute | solution.py:56
  168.8 5.1 collective-permute-done.2
  173.8 1.1 fusion.44
  175.1 0.6 multiply_subtract_fusion
  176.6 0.8 slice-done.8
  177.3 0.9 slice-done.9
  178.2 4.7 fusion.24
  183.0 9.0 %reduce-scatter.7.cloned.1.call-done = f32[2,2,8,1024]{3,2,0,1:T(8,128)} async-done(((f32[2,2,128,1024]{3,2,0,1:T(8,128)}), f32[2,2,8,1024]{3,2,0,1:T(8,128)}) %reduce-scatter.7.cloned.1.call-update) | async-done | bytes 131088 | tf_op jit(solution)/shard_map/reduce_scatter | solution.py:101
  192.0 0.9 bitcast_dynamic-update-slice_fusion.5
  192.9 73.0 %reduce-scatter.9.cloned.1.call-done = f32[2,2,8,1024]{3,2,0,1:T(8,128)} async-done(((f32[2,2,128,1024]{3,2,0,1:T(8,128)}), f32[2,2,8,1024]{3,2,0,1:T(8,128)}) %reduce-scatter.9.cloned.1.call-update) | async-done | bytes 131088 | tf_op jit(solution)/shard_map/reduce_scatter | solution.py:101
  265.9 0.9 bitcast_dynamic-update-slice_fusion.4
  266.8 72.9 %reduce-scatter.11.cloned.1.call-done = f32[2,2,8,1024]{3,2,0,1:T(8,128)} async-done(((f32[2,2,128,1024]{3,2,0,1:T(8,128)}), f32[2,2,8,1024]{3,2,0,1:T(8,128)}) %reduce-scatter.11.cloned.1.call-update) | async-done | bytes 131088 | tf_op jit(solution)/shard_map/reduce_scatter | solution.py:101
  339.7 0.9 bitcast_dynamic-update-slice_fusion.3
  340.6 72.8 %reduce-scatter.13.cloned.1.call-done = f32[2,2,8,1024]{3,2,0,1:T(8,128)} async-done(((f32[2,2,128,1024]{3,2,0,1:T(8,128)}), f32[2,2,8,1024]{3,2,0,1:T(8,128)}) %reduce-scatter.13.cloned.1.call-update) | async-done | bytes 131088 | tf_op jit(solution)/shard_map/reduce_scatter | solution.py:101
  413.3 0.9 bitcast_dynamic-update-slice_fusion.2
  414.3 72.7 %reduce-scatter.15.cloned.1.call-done = f32[2,2,8,1024]{3,2,0,1:T(8,128)} async-done(((f32[2,2,128,1024]{3,2,0,1:T(8,128)}), f32[2,2,8,1024]{3,2,0,1:T(8,128)}) %reduce-scatter.15.cloned.1.call-update) | async-done | bytes 131088 | tf_op jit(solution)/shard_map/reduce_scatter | solution.py:101
  487.0 0.9 bitcast_dynamic-update-slice_fusion.1
  487.9 72.8 %reduce-scatter.17.cloned.1.call-done = f32[2,2,8,1024]{3,2,0,1:T(8,128)} async-done(((f32[2,2,128,1024]{3,2,0,1:T(8,128)}), f32[2,2,8,1024]{3,2,0,1:T(8,128)}) %reduce-scatter.17.cloned.1.call-update) | async-done | bytes 131088 | tf_op jit(solution)/shard_map/reduce_scatter | solution.py:101
  560.7 0.9 bitcast_dynamic-update-slice_fusion
  561.6 1.0 convolution_multiply_fusion
  562.7 1.3 copy.50
  (185 shorter events, 13.1 us)
Async XLA Ops:
  11.2 93.7 %all-to-all-start = ((bf16[8,128,3,2,512]{4,1,3,2,0:T(8,128)(2,1)}), bf16[8,128,3,2,512]{4,1,3,2,0:T(8,128)(2,1)}, u32[]{:S(2)}, u32[]{:S(2)}) async-start(bf16[8,128,3,2,512]{4,1,3,2,0:T(8,128)(2,1)} %stack.151), calls=%async_computation | async-start | bytes 12582912 | tf_op jit(solution)/shard_map/all_to_all | solution.py:46
  17.2 1.0 copy-start.8
  17.2 174.8 %reduce-scatter.7.cloned.1.call-start = ((), (), s32[]{:S(2)}) async-start(), calls=%async_computation.7 | async-start | bytes 2228224 | tf_op jit(solution)/shard_map/reduce_scatter | solution.py:101
  18.2 5.9 %copy-start.27 = (s32[2,3]{1,0:T(2,128)S(1)}, s32[2,3]{1,0:T(2,128)}, u32[]{:S(2)}) copy-start(s32[2,3]{1,0:T(2,128)} %param.7) | copy-start | bytes 76
  18.2 113.4 %collective-permute-start.1 = (bf16[128,3,2,256]{3,0,2,1:T(8,128)(2,1)}, bf16[128,3,2,256]{3,0,2,1:T(8,128)(2,1)}, u32[]{:S(2)}, u32[]{:S(2)}) collective-permute-start(bf16[128,3,2,256]{3,0,2,1:T(8,128)(2,1)} %get-tuple-element.76), channel_id=1, source_target_pairs={{0,1},{1,2},{2,3},{3,4},{4,5},{5,6},{6,7},{7,8},{8,9},{9,10},{10,1... | collective-permute-start | bytes 1179656 | tf_op jit(solution)/shard_map/ppermute | solution.py:55
  18.8 111.2 %collective-permute-start = (f32[3,3,2,256]{3,2,1,0:T(2,128)}, f32[3,3,2,256]{3,2,1,0:T(2,128)}, u32[]{:S(2)}, u32[]{:S(2)}) collective-permute-start(f32[3,3,2,256]{3,2,1,0:T(2,128)} %slice_bitcast_fusion.47), channel_id=1, source_target_pairs={{0,1},{1,2},{2,3},{3,4},{4,5},{5,6},{6,7},{7,8},{8,9},{9,10},{10,1... | collective-permute-start | bytes 55304 | tf_op jit(solution)/shard_map/ppermute | solution.py:54
  23.4 7.3 %copy-start.4 = (f32[3,3,2,512]{3,2,1,0:T(2,128)}, f32[3,3,2,512]{3,2,1,0:T(2,128)S(1)}, u32[]{:S(2)}) copy-start(f32[3,3,2,512]{3,2,1,0:T(2,128)S(1)} %get-tuple-element.123) | copy-start | bytes 110596
  23.6 7.1 %copy-start.26 = (pred[512]{0:T(512)(128)(4,1)}, pred[512]{0:T(512)(128)(4,1)S(1)}, u32[]{:S(2)}) copy-start(pred[512]{0:T(512)(128)(4,1)S(1)} %broadcast_compare_fusion.1) | copy-start | bytes 1540
  104.9 6.3 %copy-start.1 = (bf16[1,2,128,3,2,512]{5,2,4,3,1,0:T(8,128)(2,1)S(1)}, bf16[1,2,128,3,2,512]{5,2,4,3,1,0:T(8,128)(2,1)}, u32[]{:S(2)}) copy-start(bf16[1,2,128,3,2,512]{5,2,4,3,1,0:T(8,128)(2,1)} %get-tuple-element.82) | copy-start | bytes 4718596
  104.9 6.3 %copy-start.2 = (bf16[1,2,128,3,2,512]{5,2,4,3,1,0:T(8,128)(2,1)S(1)}, bf16[1,2,128,3,2,512]{5,2,4,3,1,0:T(8,128)(2,1)}, u32[]{:S(2)}) copy-start(bf16[1,2,128,3,2,512]{5,2,4,3,1,0:T(8,128)(2,1)} %get-tuple-element.83) | copy-start | bytes 4718596
  108.6 2.6 copy-start
  116.0 0.7 copy-start.9
  116.0 0.7 copy-start.25
  116.0 0.8 copy-start.6
  116.0 1.4 copy-start.24
  116.0 2.1 copy-start.20
  116.0 149.8 %reduce-scatter.9.cloned.1.call-start = ((), (), s32[]{:S(2)}) async-start(), calls=%async_computation.8 | async-start | bytes 2228224 | tf_op jit(solution)/shard_map/reduce_scatter | solution.py:101
  121.4 0.7 copy-start.15
  121.4 0.7 copy-start.16
  121.4 0.7 copy-start.17
  121.5 1.2 copy-start.12
  122.1 2.2 slice-start
  123.0 2.2 slice-start.1
  129.9 0.7 copy-start.11
  129.9 1.6 copy-start.3
  130.0 209.7 %reduce-scatter.11.cloned.1.call-start = ((), (), s32[]{:S(2)}) async-start(), calls=%async_computation.9 | async-start | bytes 2228224 | tf_op jit(solution)/shard_map/reduce_scatter | solution.py:101
  132.7 0.8 copy-start.13
  132.9 2.3 slice-start.2
  133.8 2.4 slice-start.3
  141.0 0.7 copy-start.10
  141.0 0.8 copy-start.19
  141.0 0.8 copy-start.18
  141.0 0.8 copy-start.23
  141.0 0.9 copy-start.5
  141.0 0.9 copy-start.7
  141.0 272.3 %reduce-scatter.13.cloned.1.call-start = ((), (), s32[]{:S(2)}) async-start(), calls=%async_computation.10 | async-start | bytes 2228224 | tf_op jit(solution)/shard_map/reduce_scatter | solution.py:101
  142.1 0.7 copy-start.14
  142.8 2.2 slice-start.4
  143.6 2.2 slice-start.5
  150.6 0.7 copy-start.22
  150.6 336.4 %reduce-scatter.15.cloned.1.call-start = ((), (), s32[]{:S(2)}) async-start(), calls=%async_computation.11 | async-start | bytes 2228224 | tf_op jit(solution)/shard_map/reduce_scatter | solution.py:101
  151.6 2.3 slice-start.6
  152.5 2.5 slice-start.7
  159.7 9.0 %copy-start.21 = (f32[2,512]{1,0:T(2,128)S(1)}, f32[2,512]{1,0:T(2,128)}, u32[]{:S(2)}) copy-start(f32[2,512]{1,0:T(2,128)} %get-tuple-element.11) | copy-start | bytes 12292
  159.7 400.9 %reduce-scatter.17.cloned.1.call-start = ((), (), s32[]{:S(2)}) async-start(), calls=%async_computation.12 | async-start | bytes 2228224 | tf_op jit(solution)/shard_map/reduce_scatter | solution.py:101
  159.8 14.0 %collective-permute-start.2 = (bf16[128,3,2,256]{3,0,2,1:T(8,128)(2,1)S(1)}, bf16[128,3,2,256]{3,0,2,1:T(8,128)(2,1)S(1)}, u32[]{:S(2)}, u32[]{:S(2)}) collective-permute-start(bf16[128,3,2,256]{3,0,2,1:T(8,128)(2,1)S(1)} %copy-done.3), channel_id=1, source_target_pairs={{1,0},{2,1},{3,2},{4,3},{5,4},{6,5},{7,6},{8,7},{9,8},{10,9},{11,1... | collective-permute-start | bytes 1179656 | tf_op jit(solution)/shard_map/ppermute | solution.py:56
  175.1 2.2 slice-start.8
  176.0 2.2 slice-start.9
  183.0 378.6 %copy-start.28 = (s32[6]{0:T(128)S(1)}, s32[6]{0:T(128)}, u32[]{:S(2)}) copy-start(s32[6]{0:T(128)} %param.6) | copy-start | bytes 76
Sparse Core Ops, SparseCore 0:
  116.1 75.7 reduce-scatter.6
  195.9 69.8 reduce-scatter.8
  269.8 69.8 reduce-scatter.10
  343.5 69.8 reduce-scatter.12
  417.1 69.8 reduce-scatter.14
  490.8 69.8 reduce-scatter.16
